TPU v7x, 512 devices: a whole 4x4x16 slice. The times are simulated.
512 devices in a mesh: seq: 16 (over y, x), mp: 32 (over z, core).
Axes of the slice: x: 4, y: 4, z: 16, core: 2. Of those that a mesh axis runs over, the one named last changes fastest.
Arguments:
- q_proj: bfloat16 [4096, 8192], P('seq', 'mp'), may hold values from -6 to 6
- k_proj: bfloat16 [4096, 8192], P('seq', 'mp'), may hold values from -6 to 6
- v_proj: bfloat16 [4096, 8192], P('seq', 'mp'), may hold values from -6 to 6
- out_grad: bfloat16 [4096, 8192], P('seq', 'mp'), may hold values from -0.75 to 0.75
- out_weight: bfloat16 [8192, 8192], P('mp', 'seq'), may hold values from -0.0625 to 0.0625
- taps: float32 [7, 512], P(None, 'mp'), may hold values from -2.4 to 2.4
Outputs:
- grad_q: bfloat16 [4096, 8192], P('seq', 'mp')
- grad_k: bfloat16 [4096, 8192], P('seq', 'mp')
- grad_v: bfloat16 [4096, 8192], P('seq', 'mp')
- grad_weight: float32 [8192, 8192], P('mp', 'seq')
- grad_taps: float32 [7, 512], P(None, 'mp')
All inputs are finite; a program needn't handle non-finite values.
Results may differ from a plain program's by a relative error of at most 0.0029.
Values may be sent and summed in bfloat16 or wider, within the bound.
A program may use at most 64 MiB of HBM per device.

v0:
```python
import jax
import jax.numpy as jnp
from jax import lax
from jax.sharding import PartitionSpec as P

TAPS = 7
GROUP = 16


def passed_along(array, axis, by):
    count = lax.axis_size(axis)
    pairs = [(i, i + by) for i in range(count) if 0 <= i + by < count]
    return lax.ppermute(array, axis, pairs)


def shards(q_proj, k_proj, v_proj, out_grad, out_weight, taps):
    tokens, channels = q_proj.shape
    rim_rows = TAPS - 1
    q_full = q_proj.astype(jnp.float32)
    k_full = k_proj.astype(jnp.float32)
    v_full = v_proj.astype(jnp.float32)
    spread = jnp.broadcast_to(taps[:, :, None], (TAPS, taps.shape[1], GROUP)).reshape(
        TAPS, channels
    )
    tail_rows = jnp.stack([k_proj[tokens - rim_rows :], v_proj[tokens - rim_rows :]])
    before = passed_along(tail_rows, "seq", 1)
    keys_wide = jnp.concatenate([before[0], k_proj], 0).astype(jnp.float32)
    values_wide = jnp.concatenate([before[1], v_proj], 0).astype(jnp.float32)
    product = keys_wide * values_wide
    filtered = jnp.zeros((tokens, channels), jnp.float32)
    for offset in range(TAPS):
        filtered = (
            filtered + spread[offset] * product[rim_rows - offset : rim_rows - offset + tokens]
        )
    gated = (q_full * filtered).astype(jnp.bfloat16)
    seq_count, mp_count = (lax.axis_size("seq"), lax.axis_size("mp"))
    cores = mp_count // seq_count
    pairs = [
        (t * mp_count + cores * z + c, z * mp_count + cores * t + c)
        for t in range(seq_count)
        for z in range(seq_count)
        for c in range(cores)
    ]
    crossed = lax.ppermute(out_grad, ("seq", "mp"), pairs)
    tiles = lax.all_gather(crossed, "mp", axis=0)
    columns = (
        tiles.reshape(seq_count, cores, tokens, channels)
        .transpose(0, 2, 1, 3)
        .reshape(seq_count * tokens, cores * channels)
    )
    partial = lax.dot_general(
        columns, out_weight, (((1,), (1,)), ((), ())), preferred_element_type=jnp.float32
    )
    grad_gated = lax.psum_scatter(partial, "seq", scatter_dimension=0, tiled=True)
    grad_weight = lax.dot_general(
        lax.all_gather(gated, "seq", axis=0, tiled=True),
        columns,
        (((0,), (0,)), ((), ())),
        preferred_element_type=jnp.float32,
    )
    grad_q = (grad_gated * filtered).astype(jnp.bfloat16)
    grad_filtered = grad_gated * q_full
    following = passed_along(grad_filtered[:rim_rows], "seq", -1)
    grad_ext = jnp.concatenate([grad_filtered, following], 0)
    grad_product = jnp.zeros((tokens, channels), jnp.float32)
    for offset in range(TAPS):
        grad_product = grad_product + spread[offset] * grad_ext[offset : offset + tokens]
    grad_k = (grad_product * v_full).astype(jnp.bfloat16)
    grad_v = (grad_product * k_full).astype(jnp.bfloat16)
    filter_terms = jnp.stack(
        [
            jnp.sum(grad_filtered * product[rim_rows - offset : rim_rows - offset + tokens], 0)
            for offset in range(TAPS)
        ]
    )
    filter_local = filter_terms.reshape(TAPS, channels // GROUP, GROUP).sum(-1)
    grad_taps = lax.psum(filter_local, "seq")
    return (grad_q, grad_k, grad_v, grad_weight, grad_taps)


def solution(mesh):
    placed = (
        P("seq", "mp"),
        P("seq", "mp"),
        P("seq", "mp"),
        P("seq", "mp"),
        P("mp", "seq"),
        P(None, "mp"),
    )
    return jax.shard_map(
        shards,
        mesh=mesh,
        in_specs=placed,
        out_specs=(P("seq", "mp"), P("seq", "mp"), P("seq", "mp"), P("mp", "seq"), P(None, "mp")),
        check_vma=False,
    )
```

profile of v0, /device:TPU:32, one launch (start us, length us, event | category | flops | bytes accessed | tf_op | source)
XLA Modules:
  0.0 327.7 jit_solution(6569584320959466278)
XLA Ops:
  7.2 0.0 copy-start
  7.2 0.0 all-gather.6.cloned.1.call-start
  7.2 3.1 collective-permute-start
  10.3 12.5 %collective-permute-done = bf16[256,256]{1,0:T(8,128)(2,1)S(1)} collective-permute-done((bf16[256,256]{1,0:T(8,128)(2,1)}, bf16[256,256]{1,0:T(8,128)(2,1)S(1)}, u32[]{:S(2)}, u32[]{:S(2)}) %collective-permute-start) | collective-permute-done | bytes 131104 | tf_op jit(solution)/shard_map/ppermute | solution.py:44
  22.8 0.0 copy-start.5
  22.8 0.7 copy-done.5
  23.5 0.0 all-gather.6.cloned.1.call-update
  23.5 0.0 all-gather.4.cloned.1.call-start
  23.5 0.7 slice_bitcast_fusion.2
  24.3 1.3 collective-permute-start.1
  25.6 0.9 slice_bitcast_fusion.10
  26.5 0.1 broadcast_in_dim.44
  26.6 0.1 broadcast_in_dim.45
  26.7 0.1 broadcast_in_dim.42
  26.8 0.1 broadcast_in_dim.43
  26.8 0.1 broadcast_in_dim.40
  26.9 0.1 broadcast_in_dim.41
  27.0 0.1 broadcast_in_dim.38
  27.1 0.1 broadcast_in_dim.39
  27.1 0.1 broadcast_in_dim.36
  27.2 0.1 broadcast_in_dim.37
  27.3 0.1 broadcast_in_dim.34
  27.4 0.1 broadcast_in_dim.35
  27.4 0.1 broadcast_in_dim.32
  27.5 0.1 broadcast_in_dim.33
  27.6 0.0 collective-permute-done.1
  27.6 1.0 convert_multiply_fusion.2
  28.7 1.8 fusion
  30.5 0.0 all-gather.4.cloned.1.call-update
  30.5 0.0 reduce-scatter.2.cloned.1.call-start
  30.6 87.3 %all-gather.6.cloned.1.call-done = bf16[8192,256]{1,0:T(8,128)(2,1)} async-done(((bf16[256,256]{1,0:T(8,128)(2,1)}), bf16[8192,256]{1,0:T(8,128)(2,1)}) %all-gather.6.cloned.1.call-update) | async-done | bytes 4194320 | tf_op jit(solution)/shard_map/all_gather | solution.py:45
  117.8 8.0 %copy.12 = bf16[16,2,256,256]{2,0,3,1:T(8,128)(2,1)} copy(bf16[16,2,256,256]{3,2,1,0:T(8,128)(2,1)} %bitcast.36) | data formatting | bytes 8388608 | tf_op jit(solution)/shard_map/reshape | solution.py:47
  125.8 4.4 %copy.13 = bf16[64,8,16,256]{3,1,2,0:T(8,128)(2,1)S(1)} copy(bf16[64,8,16,256]{3,2,1,0:T(8,128)(2,1)} %bitcast.35) | data formatting | bytes 8388608
  130.2 0.0 copy-start.1
  130.2 2.0 copy-done.1
  132.2 0.0 copy-done
  132.2 3.2 fusion.19
  135.4 0.0 reduce-scatter.2.cloned.1.call-update
  135.4 0.0 copy-start.4
  135.4 0.0 copy-start.2
  135.4 0.0 copy-start.3
  135.5 43.0 %all-gather.4.cloned.1.call-done = bf16[4096,256]{1,0:T(8,128)(2,1)} async-done(((bf16[256,256]{1,0:T(8,128)(2,1)}), bf16[4096,256]{1,0:T(8,128)(2,1)}) %all-gather.4.cloned.1.call-update) | async-done | bytes 2097168 | tf_op jit(solution)/shard_map/all_gather | solution.py:56
  178.5 4.9 %fusion.20 = f32[256,512]{1,0:T(8,128)} fusion(bf16[4096,256]{1,0:T(8,128)(2,1)} %all-gather.4.cloned.1.call-done, bf16[4096,512]{0,1:T(8,128)(2,1)} %bitcast.34), kind=kOutput, calls=%fused_computation.61 | convolution fusion | flops 1073741824 | bytes 6815744 | tf_op jit(solution)/shard_map/dot_general | solution.py:55
  183.4 91.8 %reduce-scatter.2.cloned.1.call-done = f32[256,256]{1,0:T(8,128)} async-done(((f32[4096,256]{1,0:T(8,128)}), f32[256,256]{1,0:T(8,128)}) %reduce-scatter.2.cloned.1.call-update) | async-done | bytes 262160 | tf_op jit(solution)/shard_map/reduce_scatter | solution.py:54
  275.2 0.0 copy-done.4
  275.2 1.9 multiply_reduce_fusion
  277.1 1.3 collective-permute-start.2
  278.4 0.1 stack.36
  278.4 0.1 stack.37
  278.5 0.1 stack.38
  278.6 0.1 stack.39
  278.7 0.1 stack.40
  278.8 0.1 stack.41
  278.8 0.1 stack.42
  279.0 0.1 reduce_sum.79
  279.1 40.5 %psum.7 = f32[7,16]{1,0:T(8,128)} all-reduce(f32[7,16]{1,0:T(8,128)S(1)} %reduce_sum.79), channel_id=1, replica_groups=mesh['seq'=16,'mp'=32] {'seq'}, use_global_device_ids=true, to_apply=%region_9.0 | all-reduce | flops 112 | bytes 896 | tf_op jit(solution)/shard_map/psum | solution.py:77
  319.6 0.0 collective-permute-done.2
  319.6 0.0 copy-done.2
  319.6 0.9 multiply_convert_fusion
  320.5 0.0 copy-done.3
  320.5 0.7 multiply_convert_fusion.1
  (10 shorter events, 0.1 us)
Async XLA Ops:
  7.2 125.0 %copy-start = (bf16[256,512]{1,0:T(8,128)(2,1)S(1)}, bf16[256,512]{1,0:T(8,128)(2,1)}, u32[]{:S(2)}) copy-start(bf16[256,512]{1,0:T(8,128)(2,1)} %param.10) | copy-start | bytes 786436
  7.2 110.7 %all-gather.6.cloned.1.call-start = ((), (), s32[]{:S(2)}) async-start(), calls=%async_computation.3 | async-start | bytes 4325376 | tf_op jit(solution)/shard_map/all_gather | solution.py:45
  7.2 15.6 %collective-permute-start = (bf16[256,256]{1,0:T(8,128)(2,1)}, bf16[256,256]{1,0:T(8,128)(2,1)S(1)}, u32[]{:S(2)}, u32[]{:S(2)}) collective-permute-start(bf16[256,256]{1,0:T(8,128)(2,1)} %param.9), channel_id=1, source_target_pairs={{0,0},{1,1},{2,32},{3,33},{4,64},{5,65},{6,96},{7,97},{8,128},{9,1... | collective-permute-start | bytes 393224 | tf_op jit(solution)/shard_map/ppermute | solution.py:44
  22.8 0.7 copy-start.5
  23.5 155.0 %all-gather.4.cloned.1.call-start = ((), (), s32[]{:S(2)}) async-start(), calls=%async_computation.2 | async-start | bytes 2228224 | tf_op jit(solution)/shard_map/all_gather | solution.py:56
  24.3 3.3 %collective-permute-start.1 = (bf16[2,6,256]{2,1,0:T(8,128)(2,1)S(1)}, bf16[2,6,256]{2,1,0:T(8,128)(2,1)S(1)}, u32[]{:S(2)}, u32[]{:S(2)}) collective-permute-start(bf16[2,6,256]{2,1,0:T(8,128)(2,1)S(1)} %pad_maximum_fusion.1), channel_id=1, source_target_pairs={{0,32},{32,64},{64,96},{96,128},{128,160},{160,192},{192,224},{224... | collective-permute-start | bytes 18440 | tf_op jit(solution)/shard_map/ppermute | solution.py:13
  30.5 244.7 %reduce-scatter.2.cloned.1.call-start = ((), (), s32[]{:S(2)}) async-start(), calls=%async_computation.1 | async-start | bytes 4456448 | tf_op jit(solution)/shard_map/reduce_scatter | solution.py:54
  130.2 2.0 copy-start.1
  135.4 139.8 %copy-start.4 = (bf16[256,256]{1,0:T(8,128)(2,1)S(1)}, bf16[256,256]{1,0:T(8,128)(2,1)}, u32[]{:S(2)}) copy-start(bf16[256,256]{1,0:T(8,128)(2,1)} %param.6) | copy-start | bytes 393220
  135.4 184.1 %copy-start.2 = (bf16[256,256]{1,0:T(8,128)(2,1)S(1)}, bf16[256,256]{1,0:T(8,128)(2,1)}, u32[]{:S(2)}) copy-start(bf16[256,256]{1,0:T(8,128)(2,1)} %param.7) | copy-start | bytes 393220
  135.4 185.0 %copy-start.3 = (bf16[256,256]{1,0:T(8,128)(2,1)S(1)}, bf16[256,256]{1,0:T(8,128)(2,1)}, u32[]{:S(2)}) copy-start(bf16[256,256]{1,0:T(8,128)(2,1)} %param.8) | copy-start | bytes 393220
  277.1 42.5 %collective-permute-start.2 = (f32[6,256]{1,0:T(8,128)S(1)}, f32[6,256]{1,0:T(8,128)S(1)}, u32[]{:S(2)}, u32[]{:S(2)}) collective-permute-start(f32[6,256]{1,0:T(8,128)S(1)} %slice.158), channel_id=1, source_target_pairs={{32,0},{64,32},{96,64},{128,96},{160,128},{192,160},{224,192},{256... | collective-permute-start | bytes 18440 | tf_op jit(solution)/shard_map/ppermute | solution.py:13
Sparse Core Ops, SparseCore 0:
  23.6 94.1 all-gather.5
  121.4 57.0 all-gather.3
  182.7 92.4 reduce-scatter.1
where the time goes:
time: 328 us
  waiting for transfers between devices  235 us (72%)
  blocking collectives  40.5 us (12%)
  local copies, waits for them, and re-layouts  18.3 us (6%)
  between operations  13.9 us (4%)
  matrix products  8.15 us (2%)
  other arithmetic  6.39 us (2%)
  starting transfers between devices  5.76 us (2%)
    reduce_scatter x1, waiting for transfers between devices, shards(): lax.psum_scatter(partial, 'seq', scatter_dimension=0, tiled=True)  91.8 us
    all_gather x1, waiting for transfers between devices, shards(): tiles = lax.all_gather(crossed, 'mp', axis=0)  87.3 us
    all_gather x1, waiting for transfers between devices, shards(): lax.all_gather(gated, 'seq', axis=0, tiled=True)  43 us
    psum x1, blocking collectives, shards(): grad_taps = lax.psum(filter_local, 'seq')  40.5 us
    ppermute x1, waiting for transfers between devices, shards(): crossed = lax.ppermute(out_grad, ('seq', 'mp'), pairs)  12.5 us
    reshape x1, local copies, waits for them, and re-layouts, shards(): tiles.reshape(seq_count, cores, tokens, channels).transpose(0, 2, 1, 3)  7.96 us
    unnamed x19, local copies, waits for them, and re-layouts  7.08 us
  transfers between devices with their start and end apart: 6, of which 4 were waited for; matrix products, arithmetic and copies ran while one was open for 8% of the time, Pallas kernels for 0%

commit v1 on v0

--- a/solution.py
+++ b/solution.py
@@ -53,7 +53,9 @@
     )
     grad_gated = lax.psum_scatter(partial, "seq", scatter_dimension=0, tiled=True)
     grad_weight = lax.dot_general(
-        lax.all_gather(gated, "seq", axis=0, tiled=True),
+        jnp.concatenate(
+            lax.all_to_all(jnp.stack([gated] * lax.axis_size("seq")), "seq", 0, 0), axis=0
+        ),
         columns,
         (((0,), (0,)), ((), ())),
         preferred_element_type=jnp.float32,

time: 328 us -> 291 us (0.89)
  waiting for transfers between devices: 235 us -> 159 us
  blocking collectives: 40.5 us -> 82 us
    all_gather x1 -> x0, waiting for transfers between devices: 43 us -> none  [shards(): lax.all_gather(gated, 'seq', axis=0, tiled=True)]
    all_to_all x0 -> x1, blocking collectives: none -> 41.5 us  [shards(): lax.all_to_all(jnp.stack([gated] * lax.axis_size('seq')), 'seq', 0, 0)]
    reduce_scatter x1, waiting for transfers between devices: 91.8 us -> 52.4 us  [shards(): lax.psum_scatter(partial, 'seq', scatter_dimension=0, tiled=True)]
    all_gather x1, waiting for transfers between devices: 87.3 us -> 94.4 us  [shards(): tiles = lax.all_gather(crossed, 'mp', axis=0)]
    unnamed x19 -> x23, local copies, waits for them, and re-layouts: 7.08 us -> 8.01 us
  transfers between devices with their start and end apart: 6 -> 5, of which waited for: 4 -> 4; matrix products, arithmetic and copies ran while one was open for 8% -> 2% of each run, Pallas kernels for 0% -> 0%
where the time goes in v1:
time: 291 us; the launch traced here: 290 us
  waiting for transfers between devices  159 us (55%)
  blocking collectives  82 us (28%)
  local copies, waits for them, and re-layouts  17.8 us (6%)
  between operations  14.2 us (5%)
  starting transfers between devices  7.7 us (3%)
  matrix products  5.32 us (2%)
  other arithmetic  3.87 us (1%)
    all_gather x1, waiting for transfers between devices, shards(): tiles = lax.all_gather(crossed, 'mp', axis=0)  94.4 us
    reduce_scatter x1, waiting for transfers between devices, shards(): lax.psum_scatter(partial, 'seq', scatter_dimension=0, tiled=True)  52.4 us
    all_to_all x1, blocking collectives, shards(): lax.all_to_all(jnp.stack([gated] * lax.axis_size('seq')), 'seq', 0, 0)  41.5 us
    psum x1, blocking collectives, shards(): grad_taps = lax.psum(filter_local, 'seq')  40.5 us
    ppermute x1, waiting for transfers between devices, shards(): crossed = lax.ppermute(out_grad, ('seq', 'mp'), pairs)  12.4 us
    unnamed x23, local copies, waits for them, and re-layouts  8.01 us
    reshape x1, local copies, waits for them, and re-layouts, shards(): tiles.reshape(seq_count, cores, tokens, channels).transpose(0, 2, 1, 3)  7.96 us
  transfers between devices with their start and end apart: 5, of which 4 were waited for; matrix products, arithmetic and copies ran while one was open for 2% of the time, Pallas kernels for 0%

profile of v1, /device:TPU:32, one launch (start us, length us, event | category | flops | bytes accessed | tf_op | source)
XLA Modules:
  0.0 290.3 jit_solution(15166342369340379769)
XLA Ops:
  7.2 0.0 copy-start
  7.2 0.0 all-gather.3.cloned.1.call-start
  7.2 3.1 %collective-permute-start = (bf16[256,256]{1,0:T(8,128)(2,1)}, bf16[256,256]{1,0:T(8,128)(2,1)S(1)}, u32[]{:S(2)}, u32[]{:S(2)}) collective-permute-start(bf16[256,256]{1,0:T(8,128)(2,1)} %param.9), channel_id=1, source_target_pairs={{0,0},{1,1},{2,32},{3,33},{4,64},{5,65},{6,96},{7,97},{8,128},{9,1... | collective-permute-start | bytes 393224 | tf_op jit(solution)/shard_map/ppermute | solution.py:44
  10.3 12.4 %collective-permute-done = bf16[256,256]{1,0:T(8,128)(2,1)S(1)} collective-permute-done((bf16[256,256]{1,0:T(8,128)(2,1)}, bf16[256,256]{1,0:T(8,128)(2,1)S(1)}, u32[]{:S(2)}, u32[]{:S(2)}) %collective-permute-start) | collective-permute-done | bytes 131104 | tf_op jit(solution)/shard_map/ppermute | solution.py:44
  22.7 0.0 copy-start.6
  22.7 0.7 copy-done.6
  23.4 0.0 all-gather.3.cloned.1.call-update
  23.4 0.0 reduce-scatter.2.cloned.1.call-start
  23.4 94.4 %all-gather.3.cloned.1.call-done = bf16[8192,256]{1,0:T(8,128)(2,1)} async-done(((bf16[256,256]{1,0:T(8,128)(2,1)}), bf16[8192,256]{1,0:T(8,128)(2,1)}) %all-gather.3.cloned.1.call-update) | async-done | bytes 4194320 | tf_op jit(solution)/shard_map/all_gather | solution.py:45
  117.9 8.0 %copy.12 = bf16[16,2,256,256]{2,0,3,1:T(8,128)(2,1)} copy(bf16[16,2,256,256]{3,2,1,0:T(8,128)(2,1)} %bitcast.37) | data formatting | bytes 8388608 | tf_op jit(solution)/shard_map/reshape | solution.py:47
  125.8 4.4 %copy.13 = bf16[64,8,16,256]{3,1,2,0:T(8,128)(2,1)S(1)} copy(bf16[64,8,16,256]{3,2,1,0:T(8,128)(2,1)} %bitcast.36) | data formatting | bytes 8388608
  130.2 0.0 copy-start.1
  130.2 2.0 copy-done.1
  132.2 0.0 copy-done
  132.2 3.2 %fusion.19 = f32[4096,256]{1,0:T(8,128)} fusion(bf16[4096,512]{0,1:T(8,128)(2,1)S(1)} %bitcast.34, bf16[256,512]{1,0:T(8,128)(2,1)S(1)} %copy-done), kind=kOutput, calls=%fused_computation.60 | convolution fusion | flops 1073741824 | bytes 8650752 | tf_op jit(solution)/shard_map/dot_general | solution.py:51
  135.4 0.0 copy-start.3
  135.4 0.0 copy-start.4
  135.4 0.0 copy-start.7
  135.4 0.0 copy-start.5
  135.4 0.0 reduce-scatter.2.cloned.1.call-update
  135.5 0.9 copy-done.3
  136.3 0.1 copy-done.4
  136.4 3.3 %collective-permute-start.1 = (bf16[2,6,256]{2,1,0:T(8,128)(2,1)S(1)}, bf16[2,6,256]{2,1,0:T(8,128)(2,1)S(1)}, u32[]{:S(2)}, u32[]{:S(2)}) collective-permute-start(bf16[2,6,256]{2,1,0:T(8,128)(2,1)S(1)} %pad_maximum_fusion.1), channel_id=1, source_target_pairs={{0,32},{32,64},{64,96},{96,128},{128,160},{160,192},{192,224},{224... | collective-permute-start | bytes 18440 | tf_op jit(solution)/shard_map/ppermute | solution.py:13
  139.7 0.0 copy-done.7
  139.7 0.1 broadcast_in_dim.44
  139.8 0.1 broadcast_in_dim.45
  139.9 0.1 broadcast_in_dim.42
  139.9 0.1 broadcast_in_dim.43
  140.0 0.1 broadcast_in_dim.40
  140.1 0.1 broadcast_in_dim.41
  140.2 0.1 broadcast_in_dim.38
  140.2 0.1 broadcast_in_dim.39
  140.3 0.1 broadcast_in_dim.36
  140.4 0.1 broadcast_in_dim.37
  140.5 0.1 broadcast_in_dim.34
  140.5 0.1 broadcast_in_dim.35
  140.6 0.1 broadcast_in_dim.32
  140.7 0.1 broadcast_in_dim.33
  140.8 0.3 collective-permute-done.1
  141.0 0.1 convert_multiply_fusion.2
  141.1 0.0 copy-done.5
  141.1 0.0 copy-start.2
  141.1 0.2 fusion
  141.4 0.2 stack.27
  141.6 41.5 %all_to_all.5 = bf16[16,256,256]{2,1,0:T(8,128)(2,1)S(1)} all-to-all(bf16[16,256,256]{2,1,0:T(8,128)(2,1)S(1)} %stack.27), channel_id=1, replica_groups=mesh['seq'=16,'mp'=32] {'seq'}, dimensions={0} | all-to-all | bytes 4194304 | tf_op jit(solution)/shard_map/all_to_all | solution.py:57
  183.1 0.0 copy-done.2
  183.1 2.1 fusion.20
  185.2 52.4 %reduce-scatter.2.cloned.1.call-done = f32[256,256]{1,0:T(8,128)} async-done(((f32[4096,256]{1,0:T(8,128)}), f32[256,256]{1,0:T(8,128)}) %reduce-scatter.2.cloned.1.call-update) | async-done | bytes 262160 | tf_op jit(solution)/shard_map/reduce_scatter | solution.py:54
  237.5 1.9 multiply_reduce_fusion
  239.4 1.3 collective-permute-start.2
  240.7 0.1 stack.56
  240.8 0.1 stack.57
  240.8 0.1 stack.58
  240.9 0.1 stack.59
  241.0 0.1 stack.60
  241.1 0.1 stack.61
  241.1 0.1 stack.62
  241.3 0.1 reduce_sum.79
  241.4 40.5 %psum.7 = f32[7,16]{1,0:T(8,128)} all-reduce(f32[7,16]{1,0:T(8,128)S(1)} %reduce_sum.79), channel_id=1, replica_groups=mesh['seq'=16,'mp'=32] {'seq'}, use_global_device_ids=true, to_apply=%region_9.0 | all-reduce | flops 112 | bytes 896 | tf_op jit(solution)/shard_map/psum | solution.py:79
  281.9 0.0 collective-permute-done.2
  281.9 0.9 multiply_convert_fusion
  282.8 0.7 multiply_convert_fusion.1
  (12 shorter events, 0.1 us)
Async XLA Ops:
  7.2 125.0 %copy-start = (bf16[256,512]{1,0:T(8,128)(2,1)S(1)}, bf16[256,512]{1,0:T(8,128)(2,1)}, u32[]{:S(2)}) copy-start(bf16[256,512]{1,0:T(8,128)(2,1)} %param.10) | copy-start | bytes 786436
  7.2 110.7 %all-gather.3.cloned.1.call-start = ((), (), s32[]{:S(2)}) async-start(), calls=%async_computation.3 | async-start | bytes 4325376 | tf_op jit(solution)/shard_map/all_gather | solution.py:45
  7.2 15.5 %collective-permute-start = (bf16[256,256]{1,0:T(8,128)(2,1)}, bf16[256,256]{1,0:T(8,128)(2,1)S(1)}, u32[]{:S(2)}, u32[]{:S(2)}) collective-permute-start(bf16[256,256]{1,0:T(8,128)(2,1)} %param.9), channel_id=1, source_target_pairs={{0,0},{1,1},{2,32},{3,33},{4,64},{5,65},{6,96},{7,97},{8,128},{9,1... | collective-permute-start | bytes 393224 | tf_op jit(solution)/shard_map/ppermute | solution.py:44
  22.7 0.7 copy-start.6
  23.4 214.1 %reduce-scatter.2.cloned.1.call-start = ((), (), s32[]{:S(2)}) async-start(), calls=%async_computation.2 | async-start | bytes 4456448 | tf_op jit(solution)/shard_map/reduce_scatter | solution.py:54
  130.2 2.0 copy-start.1
  135.4 0.9 copy-start.3
  135.4 1.0 copy-start.4
  135.4 4.3 %copy-start.7 = (f32[7,16]{1,0:T(8,128)S(1)}, f32[7,16]{1,0:T(8,128)}, u32[]{:S(2)}) copy-start(f32[7,16]{1,0:T(8,128)} %param.11) | copy-start | bytes 1348
  135.4 5.7 %copy-start.5 = (bf16[256,256]{1,0:T(8,128)(2,1)S(1)}, bf16[256,256]{1,0:T(8,128)(2,1)}, u32[]{:S(2)}) copy-start(bf16[256,256]{1,0:T(8,128)(2,1)} %param.6) | copy-start | bytes 393220
  136.4 4.6 %collective-permute-start.1 = (bf16[2,6,256]{2,1,0:T(8,128)(2,1)S(1)}, bf16[2,6,256]{2,1,0:T(8,128)(2,1)S(1)}, u32[]{:S(2)}, u32[]{:S(2)}) collective-permute-start(bf16[2,6,256]{2,1,0:T(8,128)(2,1)S(1)} %pad_maximum_fusion.1), channel_id=1, source_target_pairs={{0,32},{32,64},{64,96},{96,128},{128,160},{160,192},{192,224},{224... | collective-permute-start | bytes 18440 | tf_op jit(solution)/shard_map/ppermute | solution.py:13
  141.1 41.9 %copy-start.2 = (bf16[64,8,16,256]{3,1,2,0:T(8,128)(2,1)S(1)}, bf16[64,8,16,256]{3,1,2,0:T(8,128)(2,1)}, u32[]{:S(2)}) copy-start(bf16[64,8,16,256]{3,1,2,0:T(8,128)(2,1)} %copy-done.1) | copy-start | bytes 12582916
  239.4 42.5 %collective-permute-start.2 = (f32[6,256]{1,0:T(8,128)S(1)}, f32[6,256]{1,0:T(8,128)S(1)}, u32[]{:S(2)}, u32[]{:S(2)}) collective-permute-start(f32[6,256]{1,0:T(8,128)S(1)} %slice.158), channel_id=1, source_target_pairs={{32,0},{64,32},{96,64},{128,96},{160,128},{192,160},{224,192},{256... | collective-permute-start | bytes 18440 | tf_op jit(solution)/shard_map/ppermute | solution.py:13
Sparse Core Ops, SparseCore 0:
  23.5 94.3 all-gather.2
  135.6 101.8 reduce-scatter.1
